TPU v7x, 32 devices: a whole 2x2x4 slice. The times are simulated.
32 devices in a mesh: groups: 2 (over x), row: 16 (over z, y, core).
Axes of the slice: x: 2, y: 2, z: 4, core: 2. Of those that a mesh axis runs over, the one named last changes fastest.
Arguments:
- factor_panel: bfloat16 [32768, 2048], P(('groups', 'row')), parts along dimension 0, may hold values from -0.25 to 0.25
- pivots: float32 [4096], P('groups'), parts along dimension 0, may hold values from 1 to 1.25
- right_sides: float32 [32768, 256], P(('groups', 'row')), parts along dimension 0, may hold values from -6 to 6
- block_home: int32 [32], replicated, may hold values from 0 to 31, each once
Outputs:
- remainder: float32 [32768, 256], P('groups', 'row'), parts along dimension 0
- psf_variance: float32 [512], P(('groups', 'row')), parts along dimension 0
There are 2 independent parts, one for each index of `groups`. A program takes and returns all parts, laid end to end along the dimension named above; an argument that names none is the same for every part. Nothing has to cross between parts.
Inputs may be any that keep to these rules, and one draw needn't show every extreme that they name: block_home[g] is the stored position of global block g; position p is slot p % 2 of row device p // 2; every position holds exactly one block.
All inputs are finite; a program needn't handle non-finite values.
Results may differ from a plain program's by a relative error of at most 0.0042.
Values may be sent and summed in bfloat16 or wider, within the bound.
No kernel may reach another device: no remote copies, remote signals or barrier semaphores. Data moves between devices by JAX's collectives and lax.ppermute only.
A program may use at most 128 MiB of HBM per device.

v0:
```python
import jax
import jax.numpy as jnp
from jax import lax
from jax.sharding import PartitionSpec as P

BLOCK = 512
STEPS = 4
PANEL = 2048


def spread(value, axis, source):
    kept = jnp.where(lax.axis_index(axis) == source, value, 0).astype(value.dtype)
    return lax.psum(kept, axis)


def on_device(factor_panel, pivots, right_sides, block_home):
    slot_count = factor_panel.shape[0] // BLOCK
    columns_all = right_sides.shape[1]
    row_count = lax.axis_size("row")
    row_index = lax.axis_index("row")
    block_total = block_home.shape[0]
    positions = row_index * slot_count + jnp.arange(slot_count, dtype=jnp.int32)
    global_ids = jnp.sum(
        jnp.where(
            block_home[None, :] == positions[:, None],
            jnp.arange(block_total, dtype=jnp.int32)[None, :],
            0,
        ),
        axis=1,
    )
    partial_value = right_sides.reshape(slot_count, BLOCK, columns_all)
    factor_blocks = factor_panel.reshape(slot_count, BLOCK, PANEL)
    my_columns = columns_all // row_count
    solutions = []
    for k in range(STEPS):
        slot = block_home[k] % slot_count
        rows = lax.dynamic_index_in_dim(partial_value, slot, 0, keepdims=False)
        diag_slot = block_home[k] % slot_count
        held = lax.dynamic_index_in_dim(factor_blocks, diag_slot, 0, keepdims=False)
        diag_rows = held[:, k * BLOCK : (k + 1) * BLOCK].astype(jnp.float32)
        diag_block = jnp.tril(diag_rows, -1) + jnp.diag(pivots[k * BLOCK : (k + 1) * BLOCK])
        solution = jax.scipy.linalg.solve_triangular(diag_block, rows, lower=True).astype(
            jnp.bfloat16
        )
        solution = spread(solution, "row", block_home[k] // slot_count)
        active = (global_ids > k).astype(jnp.float32)
        product = jnp.einsum(
            "sij,jc->sic",
            factor_blocks[:, :, k * BLOCK : (k + 1) * BLOCK],
            solution,
            preferred_element_type=jnp.float32,
        )
        partial_value = partial_value - active[:, None, None] * product
        partial_value = jnp.where(
            (global_ids == k)[:, None, None], solution.astype(jnp.float32)[None], partial_value
        )
        solutions.append(solution)
    stored = lax.all_to_all(
        partial_value.reshape(slot_count * BLOCK, columns_all),
        "row",
        split_axis=1,
        concat_axis=0,
        tiled=True,
    )
    ordered = jnp.take(stored.reshape(block_total, BLOCK, my_columns), block_home, axis=0)
    remainder = ordered.reshape(block_total * BLOCK, my_columns)
    solved = remainder[: STEPS * BLOCK]
    psf_variance = jnp.mean(solved * solved, axis=0)
    return (remainder, psf_variance)


def solution(mesh):
    in_specs = (P(("groups", "row"), None), P("groups"), P(("groups", "row"), None), P())
    out_specs = (P("groups", "row"), P(("groups", "row")))
    return jax.shard_map(
        on_device, mesh=mesh, in_specs=in_specs, out_specs=out_specs, check_vma=False
    )
```

profile of v0, /device:TPU:9, one launch (start us, length us, event | category | flops | bytes accessed | tf_op | source)
XLA Modules:
  0.0 519.9 jit_solution(8942205453289188810)
XLA Ops:
  7.2 1.4 fusion.108
  16.8 0.8 fusion.107
  17.5 4.6 dynamic-slice_bitcast_fusion.3
  22.1 2.0 fusion.19
  24.1 12.0 %while.8 = (s32[]{:T(128)}, f32[512,512]{1,0:T(8,128)}, s32[4,2]{0,1:T(2,128)S(1)}, f32[4,128,128]{2,1,0:T(8,128)S(1)}, s32[]{:T(128)}) while((s32[]{:T(128)}, f32[512,512]{1,0:T(8,128)}, s32[4,2]{0,1:T(2,128)S(1)}, f32[4,128,128]{2,1,0:T(8,128)S(1)}, s32[]{:T(128)}) %tuple.86), condition=%wide.while_cond, body=%wide.while_body.sunk | while | flops 2 | bytes 131181 | solution.py:42
  24.8 2.3 bitcast_dynamic-update-slice_fusion.8
  27.8 2.3 bitcast_dynamic-update-slice_fusion.8
  30.8 2.3 bitcast_dynamic-update-slice_fusion.8
  33.8 2.2 bitcast_dynamic-update-slice_fusion.8
  36.1 0.7 copy-done.2
  36.8 40.1 %custom-call.6 = f32[4,128,128]{1,2,0:T(8,128)S(1)} custom-call(f32[4,128,128]{2,1,0:T(8,128)} %copy-done.2), custom_call_target="InvertDiagBlocksLowerTriangular" | custom-call | tf_op jit(solution)/shard_map/jit(_solve_triangular)/triangular_solve | solution.py:42
  77.3 1.1 convolution_subtract_fusion.11
  78.8 1.2 convolution_subtract_fusion.7
  80.3 1.3 convolution_subtract_fusion.6
  81.9 0.8 fusion.43
  82.8 1.6 copy.57
  85.1 7.6 %while.9 = (s32[]{:T(128)}, f32[512,512]{1,0:T(8,128)S(1)}, s32[4,2]{0,1:T(2,128)S(1)}, f32[4,128,128]{2,1,0:T(8,128)S(1)}, s32[]{:T(128)}) while((s32[]{:T(128)}, f32[512,512]{1,0:T(8,128)S(1)}, s32[4,2]{0,1:T(2,128)S(1)}, f32[4,128,128]{2,1,0:T(8,128)S(1)}, s32[]{:T(128)}) %tuple.106), condition=%wide.while_cond.clone, body=%wide.while_body.clone.sunk | while | flops 2 | bytes 131181 | solution.py:42
  85.8 1.3 bitcast_dynamic-update-slice_fusion.9
  87.7 1.3 bitcast_dynamic-update-slice_fusion.9
  89.6 1.3 bitcast_dynamic-update-slice_fusion.9
  91.5 1.3 bitcast_dynamic-update-slice_fusion.9
  92.7 0.7 copy-done.3
  93.4 40.2 %custom-call.7 = f32[4,128,128]{1,2,0:T(8,128)S(1)} custom-call(f32[4,128,128]{2,1,0:T(8,128)} %copy-done.3), custom_call_target="InvertDiagBlocksLowerTriangular" | custom-call | tf_op jit(solution)/shard_map/jit(_solve_triangular)/triangular_solve | solution.py:42
  133.7 40.1 %all-reduce.5.cloned.1.call-done = bf16[512,256]{1,0:T(8,128)(2,1)} async-done(((bf16[512,256]{1,0:T(8,128)(2,1)}), bf16[512,256]{1,0:T(8,128)(2,1)}) %all-reduce.5.cloned.1.call-update) | async-done | bytes 262160 | tf_op jit(solution)/shard_map/psum | solution.py:13
  173.7 1.9 copy.55
  175.7 1.9 fusion.11
  178.2 1.1 convolution_subtract_fusion.10
  179.6 1.2 convolution_subtract_fusion.5
  181.1 1.3 convolution_subtract_fusion.4
  182.8 0.7 fusion.42
  183.8 11.1 %while.10 = (s32[]{:T(128)}, f32[512,512]{1,0:T(8,128)}, s32[4,2]{0,1:T(2,128)S(1)}, f32[4,128,128]{2,1,0:T(8,128)S(1)}, s32[]{:T(128)}) while((s32[]{:T(128)}, f32[512,512]{1,0:T(8,128)}, s32[4,2]{0,1:T(2,128)S(1)}, f32[4,128,128]{2,1,0:T(8,128)S(1)}, s32[]{:T(128)}) %tuple.107), condition=%wide.while_cond.clone.1, body=%wide.while_body.clone.1.sunk | while | flops 2 | bytes 131181 | solution.py:42
  184.4 2.2 bitcast_dynamic-update-slice_fusion.10
  187.2 2.2 bitcast_dynamic-update-slice_fusion.10
  190.0 2.2 bitcast_dynamic-update-slice_fusion.10
  192.8 2.1 bitcast_dynamic-update-slice_fusion.10
  195.5 39.3 %custom-call.8 = f32[4,128,128]{1,2,0:T(8,128)S(1)} custom-call(f32[4,128,128]{2,1,0:T(8,128)S(1)} %get-tuple-element.31), custom_call_target="InvertDiagBlocksLowerTriangular" | custom-call | tf_op jit(solution)/shard_map/jit(_solve_triangular)/triangular_solve | solution.py:42
  234.9 39.7 %all-reduce.7.cloned.1.call-done = bf16[512,256]{1,0:T(8,128)(2,1)} async-done(((bf16[512,256]{1,0:T(8,128)(2,1)}), bf16[512,256]{1,0:T(8,128)(2,1)}) %all-reduce.7.cloned.1.call-update) | async-done | bytes 262160 | tf_op jit(solution)/shard_map/psum | solution.py:13
  274.6 1.9 copy.59
  276.4 1.9 fusion.8
  279.0 1.1 convolution_subtract_fusion.9
  280.4 1.2 convolution_subtract_fusion.3
  281.9 1.3 convolution_subtract_fusion.2
  283.5 0.7 fusion.41
  284.4 8.3 %while.11 = (s32[]{:T(128)}, f32[512,512]{1,0:T(8,128)S(1)}, s32[4,2]{0,1:T(2,128)S(1)}, f32[4,128,128]{2,1,0:T(8,128)S(1)}, s32[]{:T(128)}) while((s32[]{:T(128)}, f32[512,512]{1,0:T(8,128)S(1)}, s32[4,2]{0,1:T(2,128)S(1)}, f32[4,128,128]{2,1,0:T(8,128)S(1)}, s32[]{:T(128)}) %tuple.108), condition=%wide.while_cond.clone.2, body=%wide.while_body.clone.2.sunk | while | flops 2 | bytes 131181 | solution.py:42
  285.1 1.4 bitcast_dynamic-update-slice_fusion.11
  287.1 1.4 bitcast_dynamic-update-slice_fusion.11
  289.2 1.4 bitcast_dynamic-update-slice_fusion.11
  291.3 1.4 bitcast_dynamic-update-slice_fusion.11
  293.4 39.3 %custom-call.9 = f32[4,128,128]{1,2,0:T(8,128)S(1)} custom-call(f32[4,128,128]{2,1,0:T(8,128)S(1)} %get-tuple-element.32), custom_call_target="InvertDiagBlocksLowerTriangular" | custom-call | tf_op jit(solution)/shard_map/jit(_solve_triangular)/triangular_solve | solution.py:42
  332.7 42.4 %all-reduce.9.cloned.1.call-done = bf16[512,256]{1,0:T(8,128)(2,1)} async-done(((bf16[512,256]{1,0:T(8,128)(2,1)}), bf16[512,256]{1,0:T(8,128)(2,1)}) %all-reduce.9.cloned.1.call-update) | async-done | bytes 262160 | tf_op jit(solution)/shard_map/psum | solution.py:13
  375.1 1.9 copy.62
  377.0 1.9 fusion.5
  381.4 0.7 fusion.40
  382.2 90.3 %all-reduce.11.cloned.1.call-done = bf16[512,256]{1,0:T(8,128)(2,1)} async-done(((bf16[512,256]{1,0:T(8,128)(2,1)}), bf16[512,256]{1,0:T(8,128)(2,1)}) %all-reduce.11.cloned.1.call-update) | async-done | bytes 262160 | tf_op jit(solution)/shard_map/psum | solution.py:13
  472.5 1.1 copy.65
  473.6 1.8 fusion.2
  475.4 0.8 copy.67
  476.2 1.9 all_to_all.12
  478.1 6.5 %all-to-all-start = ((f32[1024,16,16]{0,2,1:T(8,128)}), f32[1024,16,16]{0,2,1:T(8,128)S(1)}, u32[]{:S(2)}, u32[]{:S(2)}) async-start(f32[1024,16,16]{0,2,1:T(8,128)} %all_to_all.12), calls=%async_computation | async-start | bytes 2097152 | tf_op jit(solution)/shard_map/all_to_all | solution.py:58
  484.7 24.8 %all-to-all-done = f32[1024,16,16]{0,2,1:T(8,128)S(1)} async-done(((f32[1024,16,16]{0,2,1:T(8,128)}), f32[1024,16,16]{0,2,1:T(8,128)S(1)}, u32[]{:S(2)}, u32[]{:S(2)}) %all-to-all-start) | async-done | bytes 1048608 | tf_op jit(solution)/shard_map/all_to_all | solution.py:58
  509.5 0.6 copy.68
  510.3 0.6 copy.69
  510.9 0.6 gather_fusion
  512.3 1.1 broadcast_select_fusion
  (93 shorter events, 18.7 us)
Async XLA Ops:
  7.2 166.6 %all-reduce.5.cloned.1.call-start = ((), (), s32[]{:S(2)}) async-start(), calls=%async_computation.1 | async-start | bytes 524288 | tf_op jit(solution)/shard_map/psum | solution.py:13
  22.1 54.9 %copy-start.1 = (f32[1024,256]{1,0:T(8,128)S(1)}, f32[1024,256]{1,0:T(8,128)}, u32[]{:S(2)}) copy-start(f32[1024,256]{1,0:T(8,128)} %param.8) | copy-start | bytes 3145732
  24.1 60.8 %copy-start.4 = (s32[32]{0:T(128)S(1)}, s32[32]{0:T(128)}, u32[]{:S(2)}) copy-start(s32[32]{0:T(128)} %param.9) | copy-start | bytes 388
  36.1 0.7 copy-start.2
  82.7 191.8 %all-reduce.7.cloned.1.call-start = ((), (), s32[]{:S(2)}) async-start(), calls=%async_computation.2 | async-start | bytes 524288 | tf_op jit(solution)/shard_map/psum | solution.py:13
  92.7 0.7 copy-start.3
  93.4 82.2 %copy-start = (f32[512,512]{1,0:T(8,128)}, f32[512,512]{1,0:T(8,128)S(1)}, u32[]{:S(2)}) copy-start(f32[512,512]{1,0:T(8,128)S(1)} %get-tuple-element.280) | copy-start | bytes 3145732
  183.5 191.6 %all-reduce.9.cloned.1.call-start = ((), (), s32[]{:S(2)}) async-start(), calls=%async_computation.3 | async-start | bytes 524288 | tf_op jit(solution)/shard_map/psum | solution.py:13
  284.3 188.2 %all-reduce.11.cloned.1.call-start = ((), (), s32[]{:S(2)}) async-start(), calls=%async_computation.4 | async-start | bytes 524288 | tf_op jit(solution)/shard_map/psum | solution.py:13
  478.1 31.4 %all-to-all-start = ((f32[1024,16,16]{0,2,1:T(8,128)}), f32[1024,16,16]{0,2,1:T(8,128)S(1)}, u32[]{:S(2)}, u32[]{:S(2)}) async-start(f32[1024,16,16]{0,2,1:T(8,128)} %all_to_all.12), calls=%async_computation | async-start | bytes 2097152 | tf_op jit(solution)/shard_map/all_to_all | solution.py:58
Sparse Core Ops, SparseCore 0:
  82.8 90.8 all-reduce.4
  183.6 90.8 all-reduce.6
  284.4 90.6 all-reduce.8
  382.3 90.1 all-reduce.10
where the time goes:
time: 521 us; the launch traced here: 520 us
  waiting for transfers between devices  237 us (45%)
  other arithmetic  166 us (32%)
  local copies, waits for them, and re-layouts  60.9 us (12%)
  between operations  24.4 us (5%)
  matrix products  24.3 us (5%)
  starting transfers between devices  6.81 us (1%)
    psum x4, waiting for transfers between devices, spread(): return lax.psum(kept, axis)  212 us
    another operation x6, other arithmetic, on_device(): jax.scipy.linalg.solve_triangular(diag_block, rows, lower=True)  161 us
    another operation x53, local copies, waits for them, and re-layouts, on_device(): jax.scipy.linalg.solve_triangular(diag_block, rows, lower=True)  38.8 us
    all_to_all x1, waiting for transfers between devices, on_device(): lax.all_to_all(partial_value.reshape(slot_count * BLOCK, columns_all), 'r...  24.8 us
    another operation x28, matrix products, on_device(): jax.scipy.linalg.solve_triangular(diag_block, rows, lower=True)  16.7 us
  transfers between devices with their start and end apart: 5, of which 5 were waited for; matrix products, arithmetic and copies ran while one was open for 28% of the time, Pallas kernels for 0%

commit v1 on v0

--- a/solution.py
+++ b/solution.py
@@ -10,7 +10,7 @@
 
 def spread(value, axis, source):
     kept = jnp.where(lax.axis_index(axis) == source, value, 0).astype(value.dtype)
-    return lax.psum(kept, axis)
+    return lax.all_gather(kept, axis).sum(axis=0)
 
 
 def on_device(factor_panel, pivots, right_sides, block_home):

time: 521 us -> 379 us (0.73)
  waiting for transfers between devices: 237 us -> 77.5 us
  other arithmetic: 166 us -> 178 us
  matrix products: 24.3 us -> 31.4 us
    psum x4 -> x0, waiting for transfers between devices: 212 us -> none  [spread(): return lax.psum(kept, axis)]
    all_gather x0 -> x4, waiting for transfers between devices: none -> 52.7 us  [spread(): return lax.all_gather(kept, axis).sum(axis=0)]
    reduce_sum x0 -> x4, other arithmetic: none -> 11.4 us  [spread(): return lax.all_gather(kept, axis).sum(axis=0)]
    another operation x28, matrix products: 16.7 us -> 24.1 us  [on_device(): jax.scipy.linalg.solve_triangular(diag_block, rows, lower=True)]
  transfers between devices with their start and end apart: 5 -> 5, of which waited for: 5 -> 3; matrix products, arithmetic and copies ran while one was open for 28% -> 41% of each run, Pallas kernels for 0% -> 0%
where the time goes in v1:
time: 379 us; the launch traced here: 377 us
  other arithmetic  178 us (47%)
  waiting for transfers between devices  77.5 us (20%)
  local copies, waits for them, and re-layouts  61 us (16%)
  matrix products  31.4 us (8%)
  between operations  24.6 us (6%)
  starting transfers between devices  4.17 us (1%)
    another operation x6, other arithmetic, on_device(): jax.scipy.linalg.solve_triangular(diag_block, rows, lower=True)  161 us
    all_gather x4, waiting for transfers between devices, spread(): return lax.all_gather(kept, axis).sum(axis=0)  52.7 us
    another operation x53, local copies, waits for them, and re-layouts, on_device(): jax.scipy.linalg.solve_triangular(diag_block, rows, lower=True)  39.5 us
    all_to_all x1, waiting for transfers between devices, on_device(): lax.all_to_all(partial_value.reshape(slot_count * BLOCK, columns_all), 'r...  24.8 us
    another operation x28, matrix products, on_device(): jax.scipy.linalg.solve_triangular(diag_block, rows, lower=True)  24.1 us
    reduce_sum x4, other arithmetic, spread(): return lax.all_gather(kept, axis).sum(axis=0)  11.4 us
  transfers between devices with their start and end apart: 5, of which 3 were waited for; matrix products, arithmetic and copies ran while one was open for 41% of the time, Pallas kernels for 0%

profile of v1, /device:TPU:9, one launch (start us, length us, event | category | flops | bytes accessed | tf_op | source)
XLA Modules:
  0.0 376.6 jit_solution(4993105133777063047)
XLA Ops:
  7.2 1.5 fusion.108
  17.9 4.5 %dynamic-slice_bitcast_fusion.3 = (bf16[512,2048]{1,0:T(8,128)(2,1)S(1)}, bf16[512,2048]{1,0:T(8,128)(2,1)S(1)}, bf16[512,2048]{1,0:T(8,128)(2,1)S(1)}, bf16[512,2048]{1,0:T(8,128)(2,1)S(1)}) fusion(bf16[2,512,2048]{2,1,0:T(8,128)(2,1)} %bitcast.175, s32[]{:T(128)S(6)} %select_n.145, s32[]{:T(128)S(6)} %select_n.163, s32[]{:T(128)S(6)} %select_n.157, ...), kind=kLoop, calls=%fused_computation.12 | loop fusion | bytes 16777232 | tf_op jit(solution)/shard_map/jit(dynamic_index_in_dim)/squeeze | solution.py:39
  22.4 2.0 fusion.19
  24.4 7.8 %while.8 = (s32[]{:T(128)}, f32[512,512]{1,0:T(8,128)S(1)}, s32[4,2]{0,1:T(2,128)S(1)}, f32[4,128,128]{2,1,0:T(8,128)S(1)}, s32[]{:T(128)}) while((s32[]{:T(128)}, f32[512,512]{1,0:T(8,128)S(1)}, s32[4,2]{0,1:T(2,128)S(1)}, f32[4,128,128]{2,1,0:T(8,128)S(1)}, s32[]{:T(128)}) %tuple.86), condition=%wide.while_cond, body=%wide.while_body.sunk | while | flops 2 | bytes 131181 | solution.py:42
  25.0 1.3 bitcast_dynamic-update-slice_fusion.8
  27.0 1.3 bitcast_dynamic-update-slice_fusion.8
  28.9 1.3 bitcast_dynamic-update-slice_fusion.8
  30.9 1.3 bitcast_dynamic-update-slice_fusion.8
  32.2 39.3 %custom-call.6 = f32[4,128,128]{1,2,0:T(8,128)S(1)} custom-call(f32[4,128,128]{2,1,0:T(8,128)S(1)} %get-tuple-element.29), custom_call_target="InvertDiagBlocksLowerTriangular" | custom-call | tf_op jit(solution)/shard_map/jit(_solve_triangular)/triangular_solve | solution.py:42
  71.6 1.1 dynamic-slice_bitcast_fusion.4
  75.7 1.6 copy.41
  77.9 11.7 %while.9 = (s32[]{:T(128)}, f32[512,512]{1,0:T(8,128)}, s32[4,2]{0,1:T(2,128)S(1)}, f32[4,128,128]{2,1,0:T(8,128)S(1)}, s32[]{:T(128)}) while((s32[]{:T(128)}, f32[512,512]{1,0:T(8,128)}, s32[4,2]{0,1:T(2,128)S(1)}, f32[4,128,128]{2,1,0:T(8,128)S(1)}, s32[]{:T(128)}) %tuple.106), condition=%wide.while_cond.clone, body=%wide.while_body.clone.sunk | while | flops 2 | bytes 131181 | solution.py:42
  78.6 2.3 bitcast_dynamic-update-slice_fusion.9
  81.5 2.3 bitcast_dynamic-update-slice_fusion.9
  84.4 2.3 bitcast_dynamic-update-slice_fusion.9
  87.4 2.2 bitcast_dynamic-update-slice_fusion.9
  89.6 40.0 %custom-call.7 = f32[4,128,128]{1,2,0:T(8,128)} custom-call(f32[4,128,128]{2,1,0:T(8,128)S(1)} %get-tuple-element.30), custom_call_target="InvertDiagBlocksLowerTriangular" | custom-call | tf_op jit(solution)/shard_map/jit(_solve_triangular)/triangular_solve | solution.py:42
  129.8 2.9 reduce_sum.67
  132.6 0.9 copy.39
  133.5 1.9 fusion.11
  136.2 1.2 copy.42
  137.5 1.1 fusion.73
  138.6 1.1 convolution_subtract_fusion.10
  139.8 1.1 fusion.89
  140.9 1.2 convolution_subtract_fusion.5
  142.1 1.1 fusion.87
  143.3 1.3 convolution_subtract_fusion.4
  144.6 1.1 fusion.86
  147.5 11.9 %while.10 = (s32[]{:T(128)}, f32[512,512]{1,0:T(8,128)}, s32[4,2]{0,1:T(2,128)S(1)}, f32[4,128,128]{2,1,0:T(8,128)S(1)}, s32[]{:T(128)}) while((s32[]{:T(128)}, f32[512,512]{1,0:T(8,128)}, s32[4,2]{0,1:T(2,128)S(1)}, f32[4,128,128]{2,1,0:T(8,128)S(1)}, s32[]{:T(128)}) %tuple.107), condition=%wide.while_cond.clone.1, body=%wide.while_body.clone.1.sunk | while | flops 2 | bytes 131181 | solution.py:42
  148.1 2.3 bitcast_dynamic-update-slice_fusion.10
  151.1 2.3 bitcast_dynamic-update-slice_fusion.10
  154.1 2.3 bitcast_dynamic-update-slice_fusion.10
  157.1 2.2 bitcast_dynamic-update-slice_fusion.10
  159.3 39.9 %custom-call.8 = f32[4,128,128]{1,2,0:T(8,128)} custom-call(f32[4,128,128]{2,1,0:T(8,128)S(1)} %get-tuple-element.31), custom_call_target="InvertDiagBlocksLowerTriangular" | custom-call | tf_op jit(solution)/shard_map/jit(_solve_triangular)/triangular_solve | solution.py:42
  199.3 2.9 reduce_sum.68
  203.1 1.9 fusion.8
  205.2 1.1 fusion.70
  206.4 1.1 convolution_subtract_fusion.9
  207.5 1.1 fusion.85
  208.6 1.2 convolution_subtract_fusion.3
  209.8 1.1 fusion.83
  211.0 1.3 convolution_subtract_fusion.2
  212.3 1.1 fusion.82
  214.9 8.4 %while.11 = (s32[]{:T(128)}, f32[512,512]{1,0:T(8,128)S(1)}, s32[4,2]{0,1:T(2,128)S(1)}, f32[4,128,128]{2,1,0:T(8,128)S(1)}, s32[]{:T(128)}) while((s32[]{:T(128)}, f32[512,512]{1,0:T(8,128)S(1)}, s32[4,2]{0,1:T(2,128)S(1)}, f32[4,128,128]{2,1,0:T(8,128)S(1)}, s32[]{:T(128)}) %tuple.108), condition=%wide.while_cond.clone.2, body=%wide.while_body.clone.2.sunk | while | flops 2 | bytes 131181 | solution.py:42
  215.6 1.4 bitcast_dynamic-update-slice_fusion.11
  217.7 1.4 bitcast_dynamic-update-slice_fusion.11
  219.8 1.4 bitcast_dynamic-update-slice_fusion.11
  221.9 1.4 bitcast_dynamic-update-slice_fusion.11
  223.3 39.9 %custom-call.9 = f32[4,128,128]{1,2,0:T(8,128)} custom-call(f32[4,128,128]{2,1,0:T(8,128)S(1)} %get-tuple-element.32), custom_call_target="InvertDiagBlocksLowerTriangular" | custom-call | tf_op jit(solution)/shard_map/jit(_solve_triangular)/triangular_solve | solution.py:42
  263.3 3.6 all-gather.13.cloned.1.call-done
  266.8 2.9 reduce_sum.69
  270.6 1.9 fusion.5
  273.3 1.2 copy.48
  274.5 1.1 fusion.67
  276.0 1.1 fusion.81
  277.4 1.1 fusion.79
  279.0 1.1 fusion.78
  280.9 49.1 %all-gather.15.cloned.1.call-done = bf16[8192,256]{1,0:T(8,128)(2,1)} async-done(((bf16[512,256]{1,0:T(8,128)(2,1)}), bf16[8192,256]{1,0:T(8,128)(2,1)}) %all-gather.15.cloned.1.call-update) | async-done | bytes 4194320 | tf_op jit(solution)/shard_map/all_gather | solution.py:13
  330.0 2.9 reduce_sum.70
  333.0 1.7 fusion.2
  335.5 1.9 all_to_all.12
  337.4 3.8 %all-to-all-start = ((f32[1024,16,16]{0,2,1:T(8,128)}), f32[1024,16,16]{0,2,1:T(8,128)S(1)}, u32[]{:S(2)}, u32[]{:S(2)}) async-start(f32[1024,16,16]{0,2,1:T(8,128)} %all_to_all.12), calls=%async_computation | async-start | bytes 2097152 | tf_op jit(solution)/shard_map/all_to_all | solution.py:58
  341.4 24.8 %all-to-all-done = f32[1024,16,16]{0,2,1:T(8,128)S(1)} async-done(((f32[1024,16,16]{0,2,1:T(8,128)}), f32[1024,16,16]{0,2,1:T(8,128)S(1)}, u32[]{:S(2)}, u32[]{:S(2)}) %all-to-all-start) | async-done | bytes 1048608 | tf_op jit(solution)/shard_map/all_to_all | solution.py:58
  369.0 1.1 broadcast_select_fusion
  (89 shorter events, 25.5 us)
Async XLA Ops:
  7.2 122.6 %all-gather.9.cloned.1.call-start = ((), (), s32[]{:S(2)}) async-start(), calls=%async_computation.1 | async-start | bytes 4456448 | tf_op jit(solution)/shard_map/all_gather | solution.py:13
  71.5 58.0 %copy-start = (s32[32]{0:T(128)S(1)}, s32[32]{0:T(128)}, u32[]{:S(2)}) copy-start(s32[32]{0:T(128)} %param.9) | copy-start | bytes 388
  75.7 123.6 %all-gather.11.cloned.1.call-start = ((), (), s32[]{:S(2)}) async-start(), calls=%async_computation.2 | async-start | bytes 4456448 | tf_op jit(solution)/shard_map/all_gather | solution.py:13
  146.5 120.3 %all-gather.13.cloned.1.call-start = ((), (), s32[]{:S(2)}) async-start(), calls=%async_computation.3 | async-start | bytes 4456448 | tf_op jit(solution)/shard_map/all_gather | solution.py:13
  214.2 115.8 %all-gather.15.cloned.1.call-start = ((), (), s32[]{:S(2)}) async-start(), calls=%async_computation.4 | async-start | bytes 4456448 | tf_op jit(solution)/shard_map/all_gather | solution.py:13
  337.4 28.8 %all-to-all-start = ((f32[1024,16,16]{0,2,1:T(8,128)}), f32[1024,16,16]{0,2,1:T(8,128)S(1)}, u32[]{:S(2)}, u32[]{:S(2)}) async-start(f32[1024,16,16]{0,2,1:T(8,128)} %all_to_all.12), calls=%async_computation | async-start | bytes 2097152 | tf_op jit(solution)/shard_map/all_to_all | solution.py:58
Sparse Core Ops, SparseCore 0:
  75.8 52.3 all-gather.8
  146.6 52.2 all-gather.10
  214.3 52.4 all-gather.12
  281.0 48.9 all-gather.14
